TPU v7x, 32 devices: a whole 2x2x4 slice. The times are simulated.
32 devices in a mesh: dp: 2 (over core), ctx: 4 (over y, x), tp: 4 (over z).
Axes of the slice: x: 2, y: 2, z: 4, core: 2. Of those that a mesh axis runs over, the one named last changes fastest.
Arguments:
- queries: bfloat16 [4, 8192, 1536], P('dp', 'tp', 'ctx'), may hold values from -6 to 6
- key_proj: bfloat16 [4, 8192, 1536], P('dp', 'tp', 'ctx'), may hold values from -6 to 6
- value_proj: bfloat16 [4, 8192, 1536], P('dp', 'tp', 'ctx'), may hold values from -6 to 6
- grad_output: bfloat16 [4, 8192, 1536], P('dp', 'tp', 'ctx'), may hold values from -6 to 6
- filters: float32 [512, 128], P('tp'), may hold values from -0.5 to 0.5
- group_of: int32 [8192], P('tp'), may hold values from 0 to 511, as said below
Outputs:
- gated_out: bfloat16 [4, 8192, 1536], P('dp', 'tp', 'ctx')
- grad_queries: bfloat16 [4, 8192, 1536], P('dp', 'tp', 'ctx')
- grad_keys: bfloat16 [4, 8192, 1536], P('dp', 'tp', 'ctx')
- grad_values: bfloat16 [4, 8192, 1536], P('dp', 'tp', 'ctx')
- grad_filters: float32 [512, 128], P('tp')
Inputs may be any that keep to these rules, and one draw needn't show every extreme that they name: `group_of`: channels come in aligned runs of 16 consecutive channels that share one filter row, and every filter row serves exactly one run.
All inputs are finite; a program needn't handle non-finite values.
Results may differ from a plain program's by a relative error of at most 0.0058.
Values may be sent and summed in bfloat16 or wider, within the bound.
No kernel may reach another device: no remote copies, remote signals or barrier semaphores. Data moves between devices by JAX's collectives and lax.ppermute only.
A program may use at most 192 MiB of HBM per device.

v0:
```python
import jax
import jax.numpy as jnp
from jax import lax
from jax.experimental import pallas as pl
from jax.experimental.pallas import tpu as pltpu
from jax.sharding import PartitionSpec as P


WIDE = jnp.float32
NARROW = jnp.bfloat16


def wide_dot(left, right, left_dim, right_dim):
    return lax.dot_general(
        left, right, (((left_dim,), (right_dim,)), ((), ())), preferred_element_type=WIDE
    )


def circulant(filter_row):
    taps = filter_row.shape[1]
    spread = jnp.broadcast_to(filter_row, (taps, taps))
    return pltpu.roll(spread, 0, 1, stride=1, stride_axis=0)


def band_weights(h_row, hr_row):
    taps = h_row.shape[1]
    row = lax.broadcasted_iota(jnp.int32, (taps, taps), 0)
    lane = lax.broadcasted_iota(jnp.int32, (taps, taps), 1)
    turned = circulant(h_row)
    own = jnp.where(lane >= row, turned, 0.0).astype(NARROW)
    earlier = jnp.where(lane >= row, 0.0, turned).astype(NARROW)
    turned = circulant(hr_row)
    own_back = jnp.where(lane <= row, turned, 0.0).astype(NARROW)
    later = jnp.where(lane <= row, 0.0, turned).astype(NARROW)
    return jnp.concatenate([earlier, own], axis=0), jnp.concatenate([own_back, later], axis=0)


def diagonal_sum(square):
    taps = square.shape[0]
    total = square[:8]
    for a in range(8, taps, 8):
        total = total + pltpu.roll(square[a : a + 8], taps - a, 1)
    row = lax.broadcasted_iota(jnp.int32, total.shape, 0)
    for bit in (1, 2, 4):
        total = jnp.where(row & bit != 0, pltpu.roll(total, taps - bit, 1), total)
    return jnp.sum(total, axis=0, keepdims=True)


def conv_kernel(tp_size, owned, members, ids_ref, *refs):
    pieces = refs[:tp_size]
    q_ref, k_ref, v_ref, g_ref = refs[tp_size : tp_size + 4]
    gated_ref, gq_ref, gk_ref, gv_ref, h_ref, hr_ref, u_all, d_all = refs[tp_size + 4 :]
    taps = h_ref.shape[1]
    windows, channels, positions = q_ref.shape
    blocks = positions // taps
    step = pl.program_id(0)

    @pl.when(step == 0)
    def _():
        me = lax.axis_index("tp")
        group = lax.broadcasted_iota(jnp.int32, (owned, h_ref.shape[0]), 0)
        total = jnp.zeros(h_ref.shape, WIDE)
        for k in range(tp_size):
            source = lax.rem(me + tp_size - k, tp_size)
            chosen = (group + source * owned == ids_ref[...]).astype(WIDE).astype(NARROW)
            total = total + wide_dot(chosen, pieces[k][:owned, :], 0, 0)
        h_ref[...] = total
        row = lax.broadcasted_iota(jnp.int32, (taps, taps), 0)
        lane = lax.broadcasted_iota(jnp.int32, (taps, taps), 1)
        turn = (lax.rem(row + lane, taps) == 0).astype(WIDE).astype(NARROW)
        hr_ref[...] = wide_dot(total.astype(NARROW), turn, 1, 0)

    groups = channels // members
    for r in range(groups):
        rows = slice(r * members, (r + 1) * members)
        at = step * groups + r
        all_rows = pl.ds(pl.multiple_of(at * members, members), members)
        forward, backward = band_weights(h_ref[pl.ds(at, 1), :], hr_ref[pl.ds(at, 1), :])
        z_in, du_in = [], []
        for w in range(windows):
            u = k_ref[w, rows, :] * v_ref[w, rows, :]
            d = q_ref[w, rows, :] * g_ref[w, rows, :]
            u_all[w, all_rows, :] = u
            d_all[w, all_rows, :] = d
            for b in range(1, blocks):
                z_in.append(u[:, (b - 1) * taps : (b + 1) * taps])
                du_in.append(d[:, (b - 1) * taps : (b + 1) * taps])
        z = wide_dot(jnp.concatenate(z_in, axis=0), forward, 1, 0).astype(NARROW)
        du = wide_dot(jnp.concatenate(du_in, axis=0), backward, 1, 0).astype(NARROW)
        at = 0
        for w in range(windows):
            for b in range(1, blocks):
                cols = slice(b * taps, (b + 1) * taps)
                part = z[at * members : (at + 1) * members]
                gated_ref[w, rows, cols] = q_ref[w, rows, cols] * part
                gq_ref[w, rows, cols] = g_ref[w, rows, cols] * part
                cols = slice((b - 1) * taps, b * taps)
                part = du[at * members : (at + 1) * members]
                gk_ref[w, rows, cols] = v_ref[w, rows, cols] * part
                gv_ref[w, rows, cols] = k_ref[w, rows, cols] * part
                at += 1


def on_chip(arrays):
    return [pltpu.with_memory_space_constraint(a, pltpu.VMEM) for a in arrays]


def off_chip(arrays):
    return [pltpu.with_memory_space_constraint(a, pltpu.HBM) for a in arrays]


def whole_spec(shape):
    return pl.BlockSpec(shape, lambda i: (0,) * len(shape))


def conv(ids, heard, owned, queries, key_proj, value_proj, grad_output, members, step_groups=32):
    windows, channels, positions = queries.shape
    taps = heard[0].shape[1]
    here = channels // members
    block = step_groups * members
    vmem = pl.BlockSpec(memory_space=pltpu.VMEM)
    wide_spec = pl.BlockSpec((windows, block, positions), lambda i: (0, i, 0))
    big = jax.ShapeDtypeStruct(queries.shape, NARROW)
    table = jax.ShapeDtypeStruct((here, taps), WIDE)

    def kernel(*refs):
        conv_kernel(len(heard), owned, members, *refs)

    return pl.pallas_call(
        kernel,
        grid=(channels // block,),
        in_specs=[vmem] * (1 + len(heard)) + [wide_spec] * 4,
        out_specs=[wide_spec] * 4 + [whole_spec(table.shape)] * 2 + [vmem] * 2,
        out_shape=[big] * 4 + [table] * 2 + [pltpu.VMEM(big.shape, NARROW)] * 2,
        cost_estimate=pl.CostEstimate(
            flops=8 * taps * queries.size, bytes_accessed=16 * queries.size, transcendentals=0
        ),
        compiler_params=pltpu.CompilerParams(vmem_limit_bytes=40000000),
        name="conv",
    )(ids, *on_chip(heard), *off_chip((queries, key_proj, value_proj, grad_output)))


def outer_kernel(members, scale, chunk, x_ref, d_ref, u_all, d_all, out_ref, square_ref):
    even = lax.rem(lax.axis_index("ctx"), 2) == 0
    windows, _, positions = u_all.shape
    channels = out_ref.shape[0] * members
    half = windows // 2
    taps = x_ref.shape[-1]
    first = pl.program_id(0) * channels
    blocks = positions // taps
    chunks = channels // members // chunk
    slots = square_ref.shape[0]
    row = lax.broadcasted_iota(jnp.int32, (taps, taps), 0)
    lane = lax.broadcasted_iota(jnp.int32, (taps, taps), 1)
    empty = jnp.zeros((members, taps), NARROW)

    def squares(at, slot):
        for r in range(chunk):
            rows = pl.ds(pl.multiple_of(first + (at * chunk + r) * members, members), members)
            lefts, rights = [], []
            for w in range(windows):
                u = u_all[w, rows, :]
                d = d_all[w, rows, :]
                if w < half:
                    prior = jnp.where(even, d_ref[w, rows, :], x_ref[w, rows, :])
                else:
                    prior = empty
                    lefts.append(
                        jnp.where(even, x_ref[w - half, rows, :], d_ref[w - half, rows, :])
                    )
                    rights.append(jnp.concatenate([u[:, -taps:], empty], axis=1))
                for b in range(blocks):
                    lefts.append(d[:, b * taps : (b + 1) * taps])
                    if b == 0:
                        rights.append(jnp.concatenate([prior, u[:, :taps]], axis=1))
                    else:
                        rights.append(u[:, (b - 1) * taps : (b + 1) * taps])
            outer = wide_dot(jnp.concatenate(lefts, axis=0), jnp.concatenate(rights, axis=0), 0, 0)
            square_ref[slot, r] = jnp.where(lane <= row, outer[:, taps:], outer[:, :taps])

    def sums(at, slot):
        found = [diagonal_sum(square_ref[slot, r]) for r in range(chunk)]
        out_ref[at * chunk : (at + 1) * chunk, :] = jnp.concatenate(found, axis=0) * scale

    for at in range(chunks + 1):
        if at < chunks:
            squares(at, at % slots)
        if at > 0:
            sums(at - 1, (at - 1) % slots)


def outer_terms(x1, d1, u, d, members, scale, step_groups=16, chunk=8, slots=2):
    channels = u.shape[1]
    taps = x1.shape[-1]
    block = step_groups * members
    vmem = pl.BlockSpec(memory_space=pltpu.VMEM)

    def kernel(*refs):
        outer_kernel(members, scale, chunk, *refs)

    return pl.pallas_call(
        kernel,
        grid=(channels // block,),
        in_specs=[vmem] * 4,
        out_specs=pl.BlockSpec((step_groups, taps), lambda i: (i, 0)),
        out_shape=jax.ShapeDtypeStruct((channels // members, taps), WIDE),
        scratch_shapes=[pltpu.VMEM((slots, chunk, taps, taps), WIDE)],
        cost_estimate=pl.CostEstimate(
            flops=8 * taps * u.size, bytes_accessed=8 * u.size, transcendentals=0
        ),
        compiler_params=pltpu.CompilerParams(vmem_limit_bytes=20000000),
        name="outer",
    )(*on_chip((x1, d1, u, d)))


def border_kernel(members, *refs):
    x1_ref, d1_ref, x2_ref, d2_ref, u_all, h_ref, hr_ref = refs[:7]
    qh_ref, gh_ref, qt_ref, gt_ref, kt_ref, vt_ref = refs[7:13]
    gated_ref, gq_ref, gk_ref, gv_ref = refs[17:]
    even = lax.rem(lax.axis_index("ctx"), 2) == 0
    half, _, taps = x1_ref.shape
    channels = qh_ref.shape[1]
    start = pl.program_id(0) * channels
    for r in range(channels // members):
        rows = slice(r * members, (r + 1) * members)
        halo_rows = pl.ds(pl.multiple_of(start + r * members, members), members)
        forward, backward = band_weights(h_ref[r : r + 1, :], hr_ref[r : r + 1, :])
        z_in, du_in = [], []
        for w in range(2 * half):
            first = w < half
            x = (x1_ref if first else x2_ref)[w % half, rows, :]
            d = (d1_ref if first else d2_ref)[w % half, rows, :]
            z_in.append(
                jnp.concatenate([jnp.where(even, d, x), u_all[w, halo_rows, :taps]], axis=1)
            )
            x = (x2_ref if first else x1_ref)[w % half, rows, :]
            d = (d2_ref if first else d1_ref)[w % half, rows, :]
            du_in.append(
                jnp.concatenate([qt_ref[w, rows, :] * gt_ref[w, rows, :], jnp.where(even, x, d)], axis=1)
            )
        z = wide_dot(jnp.concatenate(z_in, axis=0), forward, 1, 0).astype(NARROW)
        du = wide_dot(jnp.concatenate(du_in, axis=0), backward, 1, 0).astype(NARROW)
        for w in range(2 * half):
            part = z[w * members : (w + 1) * members]
            gated_ref[w, rows, :] = qh_ref[w, rows, :] * part
            gq_ref[w, rows, :] = gh_ref[w, rows, :] * part
            part = du[w * members : (w + 1) * members]
            gk_ref[w, rows, :] = vt_ref[w, rows, :] * part
            gv_ref[w, rows, :] = kt_ref[w, rows, :] * part


def border(x1, d1, x2, d2, u, h, hr, queries, key_proj, value_proj, grad_output, outs, members, step_groups=64):
    windows, channels, positions = queries.shape
    taps = x1.shape[-1]
    block = step_groups * members
    last = positions // taps - 1
    halo = pl.BlockSpec((x1.shape[0], block, taps), lambda i: (0, i, 0))
    vmem = pl.BlockSpec(memory_space=pltpu.VMEM)
    head = pl.BlockSpec((windows, block, taps), lambda i: (0, i, 0))
    tail = pl.BlockSpec((windows, block, taps), lambda i: (0, i, last))
    rows = pl.BlockSpec((step_groups, taps), lambda i: (i, 0))
    anywhere = pl.BlockSpec(memory_space=pltpu.HBM)

    def kernel(*refs):
        border_kernel(members, *refs)

    return pl.pallas_call(
        kernel,
        grid=(channels // block,),
        in_specs=[halo] * 4 + [vmem] + [rows] * 2 + [head] * 2 + [tail] * 4 + [anywhere] * 4,
        out_specs=[head, head, tail, tail],
        out_shape=[jax.ShapeDtypeStruct(queries.shape, NARROW)] * 4,
        input_output_aliases={13: 0, 14: 1, 15: 2, 16: 3},
        cost_estimate=pl.CostEstimate(
            flops=32 * taps * x1.size, bytes_accessed=64 * x1.size, transcendentals=0
        ),
        compiler_params=pltpu.CompilerParams(vmem_limit_bytes=40000000),
        name="border",
    )(
        *off_chip((x1, d1, x2, d2)),
        *on_chip((u,)),
        h,
        hr,
        *off_chip((queries, grad_output, queries, grad_output, key_proj, value_proj, *outs)),
    )


def place_kernel(ids_refs, rows_ref, out_ref):
    me = lax.axis_index("tp")
    tp_size = len(ids_refs)
    owned, taps = out_ref.shape
    slices, _, each, _ = rows_ref.shape
    total = jnp.zeros(out_ref.shape, WIDE)
    for k in range(tp_size):
        source = lax.rem(me + tp_size - k, tp_size)
        ids = ids_refs[k][owned : owned + 16, :].astype(WIDE)
        number = (ids[0:1, :] * 256.0 + ids[1:2, :]).astype(jnp.int32)
        here = number.shape[1]
        slot = lax.broadcasted_iota(jnp.int32, (owned, here), 0) + me * owned
        chosen = (slot == number).astype(WIDE).astype(NARROW)
        piece = rows_ref[:, pl.ds(source, 1)].reshape(slices * each, taps)
        total = total + wide_dot(chosen, piece, 1, 0)
    row = lax.broadcasted_iota(jnp.int32, (taps, taps), 0)
    lane = lax.broadcasted_iota(jnp.int32, (taps, taps), 1)
    turn = (lax.rem(row + lane, taps) == 0).astype(WIDE).astype(NARROW)
    out_ref[...] = wide_dot(total.astype(NARROW), turn, 1, 0)


def shards(queries, key_proj, value_proj, grad_output, filters, group_of):
    windows, channels, positions = queries.shape
    owned, taps = filters.shape
    ctx_size, tp_size, dp_size = (lax.axis_size(a) for a in ("ctx", "tp", "dp"))
    members = channels // owned
    half = windows // 2
    even = lax.rem(lax.axis_index("ctx"), 2) == 0

    def messages(streams, u_at, d_at):
        q, k, v, g = streams
        u = k[u_at : u_at + half, :, -taps:] * v[u_at : u_at + half, :, -taps:]
        d = q[d_at : d_at + half, :, :taps] * g[d_at : d_at + half, :, :taps]
        return jnp.where(even, u, d), jnp.where(even, d, u)

    every = range(ctx_size)
    near = [(i, i ^ 1) for i in every]
    far = [(i, i + 1) for i in every if i % 2 == 1 and i + 1 < ctx_size]
    far += [(i, i - 1) for i in every if i % 2 == 0 and i > 0]

    streams = (queries, key_proj, value_proj, grad_output)
    near_1, far_1 = messages(streams, 0, half)
    x1 = lax.ppermute(near_1, "ctx", near)
    d1 = lax.ppermute(far_1, "ctx", far)

    run_ids = group_of.reshape(1, owned, members)[:, :, 0]
    id_rows = jnp.concatenate(
        [run_ids // 256, run_ids % 256, jnp.zeros((14, owned), jnp.int32)], axis=0
    ).astype(NARROW)
    sent = jnp.concatenate([filters.astype(NARROW), id_rows], axis=0)
    heard = [sent]
    for k in range(1, tp_size):
        pairs = [(i, (i + k) % tp_size) for i in range(tp_size)]
        heard.append(lax.ppermute(sent, "tp", pairs))

    *streams_2, _ = lax.optimization_barrier((*streams, near_1))
    near_2, far_2 = messages(streams_2, half, 0)
    x2 = lax.ppermute(near_2, "ctx", near)
    d2 = lax.ppermute(far_2, "ctx", far)

    *outs, h, hr, u, d = conv(
        run_ids, heard, owned, queries, key_proj, value_proj, grad_output, members
    )
    scale = 1.0 / (windows * positions * dp_size * ctx_size)
    grad = outer_terms(x1, d1, u, d, members, scale)
    outs = border(x1, d1, x2, d2, u, h, hr, queries, key_proj, value_proj, grad_output, outs, members)

    slices = dp_size * ctx_size
    each = owned // slices
    swapped = lax.all_to_all(grad, ("dp", "ctx"), 0, 0, tiled=True)
    summed = jnp.sum(swapped.reshape(slices, each, taps), axis=0).astype(NARROW)
    copies = jnp.broadcast_to(summed[None], (slices * tp_size, each, taps))
    rows = lax.all_to_all(copies, ("dp", "ctx", "tp"), 0, 0, tiled=True)
    rows = rows.reshape(slices, tp_size, each, taps)

    def kernel(*refs):
        place_kernel(refs[:tp_size], refs[tp_size], refs[tp_size + 1])

    grad_filters = pl.pallas_call(
        kernel,
        in_specs=[pl.BlockSpec(memory_space=pltpu.VMEM)] * (tp_size + 1),
        out_specs=pl.BlockSpec(memory_space=pltpu.VMEM),
        out_shape=jax.ShapeDtypeStruct((owned, taps), WIDE),
        compiler_params=pltpu.CompilerParams(vmem_limit_bytes=10000000),
        name="place",
    )(*on_chip((*heard, rows)))
    return (*outs, grad_filters)


def solution(mesh):
    data = P("dp", "tp", "ctx")
    in_specs = (data, data, data, data, P("tp", None), P("tp"))
    out_specs = (data, data, data, data, P("tp", None))

    return jax.shard_map(shards, mesh=mesh, in_specs=in_specs, out_specs=out_specs, check_vma=False)
```

profile of v0, /device:TPU:0, one launch (start us, length us, event | category | flops | bytes accessed | tf_op | source)
XLA Modules:
  0.0 71.1 jit_solution(958609730720719454)
XLA Ops:
  0.6 0.8 %reshape.163 = s32[1,128,16]{2,1,0:T(8,128)S(1)} reshape(s32[2048]{0:T(1024)} %param.11) | data formatting | bytes 16384 | tf_op jit(solution)/shard_map/reshape | solution.py:333
  1.4 0.1 slice_reduce_fusion
  1.5 0.8 %convert_element_type.11 = bf16[128,128]{1,0:T(8,128)(2,1)S(1)} convert(f32[128,128]{1,0:T(8,128)} %param.10) | non-fusion elementwise | flops 16384 | bytes 98304 | tf_op jit(solution)/shard_map/convert_element_type | solution.py:337
  2.4 0.1 pad.3.clone
  2.5 0.1 maximum_maximum_fusion.refs_1_.refs_0_
  2.6 3.1 %collective-permute-start.4 = (bf16[144,128]{1,0:T(8,128)(2,1)S(1)}, bf16[144,128]{1,0:T(8,128)(2,1)S(1)}, u32[]{:S(2)}, u32[]{:S(2)}) collective-permute-start(bf16[144,128]{1,0:T(8,128)(2,1)S(1)} %maximum_maximum_fusion.refs_1_.refs_0_), channel_id=1, source_target_pairs={{0,1},{1,2},{2,3},{3,0},{4,5},{5,6},{6,7},{7,4},{8,9},{9,10},{10,1... | collective-permute-start | bytes 110600 | tf_op jit(solution)/shard_map/ppermute | solution.py:341
  5.7 2.6 %collective-permute-start.5 = (bf16[144,128]{1,0:T(8,128)(2,1)S(1)}, bf16[144,128]{1,0:T(8,128)(2,1)S(1)}, u32[]{:S(2)}, u32[]{:S(2)}) collective-permute-start(bf16[144,128]{1,0:T(8,128)(2,1)S(1)} %maximum_maximum_fusion.refs_1_.refs_0_), channel_id=1, source_target_pairs={{0,2},{1,3},{2,0},{3,1},{4,6},{5,7},{6,4},{7,5},{8,10},{9,11},{10,... | collective-permute-start | bytes 110600 | tf_op jit(solution)/shard_map/ppermute | solution.py:341
  8.3 1.3 %collective-permute-start.6 = (bf16[144,128]{1,0:T(8,128)(2,1)S(1)}, bf16[144,128]{1,0:T(8,128)(2,1)S(1)}, u32[]{:S(2)}, u32[]{:S(2)}) collective-permute-start(bf16[144,128]{1,0:T(8,128)(2,1)S(1)} %maximum_maximum_fusion.refs_1_.refs_0_), channel_id=1, source_target_pairs={{0,3},{1,0},{2,1},{3,2},{4,7},{5,4},{6,5},{7,6},{8,11},{9,8},{10,9... | collective-permute-start | bytes 110600 | tf_op jit(solution)/shard_map/ppermute | solution.py:341
  9.6 1.6 %broadcast_select_fusion.2 = (bf16[1,2048,128]{2,1,0:T(8,128)(2,1)S(1)}, bf16[1,2048,128]{2,1,0:T(8,128)(2,1)S(1)}) fusion(pred[]{:T(512)S(6)} %eq.5, bf16[2,2048,384]{2,1,0:T(8,128)(2,1)} %refs_12_.1, bf16[2,2048,384]{2,1,0:T(8,128)(2,1)} %refs_11_.1, bf16[2,2048,384]{2,1,0:T(8,128)(2,1)} %refs_10_.1, bf16[2,2048,384]{2,1,0:T(8,128)(2,1)} %refs_9_.1), kind=kLoop, calls=%fused_computation.6 | loop fusion | flops 1048576 | bytes 3145729 | tf_op jit(solution)/shard_map/jit(_where)/select_n | solution.py:321
  11.2 1.6 %collective-permute-start = (bf16[1,2048,128]{2,1,0:T(8,128)(2,1)S(1)}, bf16[1,2048,128]{2,1,0:T(8,128)(2,1)S(1)}, u32[]{:S(2)}, u32[]{:S(2)}) collective-permute-start(bf16[1,2048,128]{2,1,0:T(8,128)(2,1)S(1)} %get-tuple-element.40), channel_id=1, source_target_pairs={{0,4},{4,0},{8,12},{12,8},{1,5},{5,1},{9,13},{13,9},{2,6},{6,2},{1... | collective-permute-start | bytes 1572872 | tf_op jit(solution)/shard_map/ppermute | solution.py:330
  12.8 0.7 collective-permute-start.1
  13.5 2.7 %broadcast_select_fusion = (bf16[1,2048,128]{2,1,0:T(8,128)(2,1)}, bf16[1,2048,128]{2,1,0:T(8,128)(2,1)}) fusion(pred[]{:T(512)S(6)} %eq.5, bf16[2,2048,384]{2,1,0:T(8,128)(2,1)} %refs_12_.1, bf16[2,2048,384]{2,1,0:T(8,128)(2,1)} %refs_11_.1, bf16[2,2048,384]{2,1,0:T(8,128)(2,1)} %refs_10_.1, bf16[2,2048,384]{2,1,0:T(8,128)(2,1)} %refs_9_.1), kind=kLoop, calls=%fused_computation.4 | loop fusion | flops 1048576 | bytes 3145729 | tf_op jit(solution)/shard_map/jit(_where)/select_n | solution.py:321
  16.1 0.0 collective-permute-done.4.refs_2_.refs_1_
  16.2 4.2 %collective-permute-start.2 = (bf16[1,2048,128]{2,1,0:T(8,128)(2,1)}, bf16[1,2048,128]{2,1,0:T(8,128)(2,1)}, u32[]{:S(2)}, u32[]{:S(2)}) collective-permute-start(bf16[1,2048,128]{2,1,0:T(8,128)(2,1)} %get-tuple-element.38), channel_id=1, source_target_pairs={{0,4},{4,0},{8,12},{12,8},{1,5},{5,1},{9,13},{13,9},{2,6},{6,2},{1... | collective-permute-start | bytes 1572872 | tf_op jit(solution)/shard_map/ppermute | solution.py:345
  20.3 0.0 collective-permute-done.5.refs_3_.refs_2_
  20.4 1.5 %collective-permute-start.3 = (bf16[1,2048,128]{2,1,0:T(8,128)(2,1)}, bf16[1,2048,128]{2,1,0:T(8,128)(2,1)}, u32[]{:S(2)}, u32[]{:S(2)}) collective-permute-start(bf16[1,2048,128]{2,1,0:T(8,128)(2,1)} %get-tuple-element.37), channel_id=1, source_target_pairs={{4,8},{8,4},{5,9},{9,5},{6,10},{10,6},{7,11},{11,7},{20,24},{24,20... | collective-permute-start | bytes 1572872 | tf_op jit(solution)/shard_map/ppermute | solution.py:346
  21.8 0.0 collective-permute-done.6.refs_4_.refs_3_
  21.8 11.0 %conv.1 = (bf16[2,2048,384]{2,1,0:T(8,128)(2,1)}, bf16[2,2048,384]{2,1,0:T(8,128)(2,1)}, bf16[2,2048,384]{2,1,0:T(8,128)(2,1)}, bf16[2,2048,384]{2,1,0:T(8,128)(...) custom-call(s32[1,128]{1,0:T(1,128)S(1)} %bitcast.11, ...), custom_call_target="tpu_custom_call" | custom-call | flops 1610612736 | bytes 25165824 | tf_op jit(solution)/shard_map/conv/pallas_call | solution.py:129
  32.8 0.0 collective-permute-done.refs_0_
  32.8 0.0 copy-start
  32.8 0.0 collective-permute-done.1.refs_1_
  32.8 0.0 copy-start.1
  32.8 6.4 %outer.1 = f32[128,128]{1,0:T(8,128)S(1)} custom-call(bf16[1,2048,128]{2,1,0:T(8,128)(2,1)S(1)} %collective-permute-done.refs_0_, bf16[1,2048,128]{2,1,0:T(8,128)(2,1)S(1)} %collective-permute-done.1.refs_1_, bf16[2,2048,384]{2,1,0:T(8,128)(2,1)S(1)} %get-tuple-element.25.refs_4_.refs_2_, bf16[2,2048,384]{2,1,0:T(8,128)(2,1)S(1)} %get-tuple-element.36.refs_3_), custom_call_target="tpu_custom_call" | custom-call | flops 1610612736 | bytes 12582912 | tf_op jit(solution)/shard_map/outer/pallas_call | solution.py:201
  39.2 0.0 copy-done
  39.2 0.0 copy-done.1
  39.2 19.1 %all_to_all.14 = f32[8,16,128]{2,1,0:T(8,128)S(1)} all-to-all(f32[8,16,128]{2,1,0:T(8,128)S(1)} %bitcast.10), channel_id=1, replica_groups=mesh['dp'=2,'ctx'=4,'tp'=4] {'dp','ctx'}, dimensions={0} | all-to-all | bytes 131072 | tf_op jit(solution)/shard_map/all_to_all | solution.py:357
  58.3 0.7 broadcast_in_dim.10
  59.0 3.2 %all-to-all-start.1 = ((bf16[32,16,128]{2,1,0:T(8,128)(2,1)}), bf16[32,16,128]{2,1,0:T(8,128)(2,1)S(1)}, u32[]{:S(2)}, u32[]{:S(2)}) async-start(bf16[32,16,128]{2,1,0:T(8,128)(2,1)} %broadcast_in_dim.10), calls=%async_computation.1 | async-start | bytes 262144 | tf_op jit(solution)/shard_map/all_to_all | solution.py:360
  62.2 0.0 collective-permute-done.2.refs_2_
  62.2 0.0 collective-permute-done.3.refs_3_
  62.2 6.3 %border.1 = (bf16[2,2048,384]{2,1,0:T(8,128)(2,1)}, bf16[2,2048,384]{2,1,0:T(8,128)(2,1)}, bf16[2,2048,384]{2,1,0:T(8,128)(2,1)}, bf16[2,2048,384]{2,1,0:T(8,128)(2,1)}) custom-call(bf16[1,2048,128]{2,1,0:T(8,128)(2,1)} %copy-done, bf16[1,2048,128]{2,1,0:T(8,128)(2,1)} %copy-done.1, ...), custom_call_target="tpu_custom_call", output_to_operand_aliasing={{0}: (13, {}), {1}: (14, {}), {2}: (15, {}), {3}: (16, {})} | custom-call | flops 1073741824 | bytes 16777216 | tf_op jit(solution)/shard_map/border/pallas_call | solution.py:267
  68.5 1.7 %all-to-all-done.1 = bf16[32,16,128]{2,1,0:T(8,128)(2,1)S(1)} async-done(((bf16[32,16,128]{2,1,0:T(8,128)(2,1)}), bf16[32,16,128]{2,1,0:T(8,128)(2,1)S(1)}, u32[]{:S(2)}, u32[]{:S(2)}) %all-to-all-start.1) | async-done | bytes 131104 | tf_op jit(solution)/shard_map/all_to_all | solution.py:360
  70.2 0.9 %place.1 = f32[128,128]{1,0:T(8,128)} custom-call(bf16[144,128]{1,0:T(8,128)(2,1)S(1)} %maximum_maximum_fusion.refs_1_.refs_0_, bf16[144,128]{1,0:T(8,128)(2,1)S(1)} %collective-permute-done.4.refs_2_.refs_1_, bf16[144,128]{1,0:T(8,128)(2,1)S(1)} %collective-permute-done.5.refs_3_.refs_2_, bf16[144,128]{1,0:T(8,128)(2,1)S(1)} %collective-permute-done.6.refs_4_.refs_3_, ...), custom_call_target="tpu_custom_call" | custom-call | tf_op jit(solution)/shard_map/place/pallas_call | solution.py:366
  (3 shorter events, 0.0 us)
Async XLA Ops:
  2.6 13.6 %collective-permute-start.4 = (bf16[144,128]{1,0:T(8,128)(2,1)S(1)}, bf16[144,128]{1,0:T(8,128)(2,1)S(1)}, u32[]{:S(2)}, u32[]{:S(2)}) collective-permute-start(bf16[144,128]{1,0:T(8,128)(2,1)S(1)} %maximum_maximum_fusion.refs_1_.refs_0_), channel_id=1, source_target_pairs={{0,1},{1,2},{2,3},{3,0},{4,5},{5,6},{6,7},{7,4},{8,9},{9,10},{10,1... | collective-permute-start | bytes 110600 | tf_op jit(solution)/shard_map/ppermute | solution.py:341
  5.7 14.7 %collective-permute-start.5 = (bf16[144,128]{1,0:T(8,128)(2,1)S(1)}, bf16[144,128]{1,0:T(8,128)(2,1)S(1)}, u32[]{:S(2)}, u32[]{:S(2)}) collective-permute-start(bf16[144,128]{1,0:T(8,128)(2,1)S(1)} %maximum_maximum_fusion.refs_1_.refs_0_), channel_id=1, source_target_pairs={{0,2},{1,3},{2,0},{3,1},{4,6},{5,7},{6,4},{7,5},{8,10},{9,11},{10,... | collective-permute-start | bytes 110600 | tf_op jit(solution)/shard_map/ppermute | solution.py:341
  8.3 13.6 %collective-permute-start.6 = (bf16[144,128]{1,0:T(8,128)(2,1)S(1)}, bf16[144,128]{1,0:T(8,128)(2,1)S(1)}, u32[]{:S(2)}, u32[]{:S(2)}) collective-permute-start(bf16[144,128]{1,0:T(8,128)(2,1)S(1)} %maximum_maximum_fusion.refs_1_.refs_0_), channel_id=1, source_target_pairs={{0,3},{1,0},{2,1},{3,2},{4,7},{5,4},{6,5},{7,6},{8,11},{9,8},{10,9... | collective-permute-start | bytes 110600 | tf_op jit(solution)/shard_map/ppermute | solution.py:341
  11.2 21.5 %collective-permute-start = (bf16[1,2048,128]{2,1,0:T(8,128)(2,1)S(1)}, bf16[1,2048,128]{2,1,0:T(8,128)(2,1)S(1)}, u32[]{:S(2)}, u32[]{:S(2)}) collective-permute-start(bf16[1,2048,128]{2,1,0:T(8,128)(2,1)S(1)} %get-tuple-element.40), channel_id=1, source_target_pairs={{0,4},{4,0},{8,12},{12,8},{1,5},{5,1},{9,13},{13,9},{2,6},{6,2},{1... | collective-permute-start | bytes 1572872 | tf_op jit(solution)/shard_map/ppermute | solution.py:330
  12.8 20.0 %collective-permute-start.1 = (bf16[1,2048,128]{2,1,0:T(8,128)(2,1)S(1)}, bf16[1,2048,128]{2,1,0:T(8,128)(2,1)S(1)}, u32[]{:S(2)}, u32[]{:S(2)}) collective-permute-start(bf16[1,2048,128]{2,1,0:T(8,128)(2,1)S(1)} %get-tuple-element.39), channel_id=1, source_target_pairs={{4,8},{8,4},{5,9},{9,5},{6,10},{10,6},{7,11},{11,7},{20,24},{24,20... | collective-permute-start | bytes 1572872 | tf_op jit(solution)/shard_map/ppermute | solution.py:331
  16.2 46.1 %collective-permute-start.2 = (bf16[1,2048,128]{2,1,0:T(8,128)(2,1)}, bf16[1,2048,128]{2,1,0:T(8,128)(2,1)}, u32[]{:S(2)}, u32[]{:S(2)}) collective-permute-start(bf16[1,2048,128]{2,1,0:T(8,128)(2,1)} %get-tuple-element.38), channel_id=1, source_target_pairs={{0,4},{4,0},{8,12},{12,8},{1,5},{5,1},{9,13},{13,9},{2,6},{6,2},{1... | collective-permute-start | bytes 1572872 | tf_op jit(solution)/shard_map/ppermute | solution.py:345
  20.4 41.9 %collective-permute-start.3 = (bf16[1,2048,128]{2,1,0:T(8,128)(2,1)}, bf16[1,2048,128]{2,1,0:T(8,128)(2,1)}, u32[]{:S(2)}, u32[]{:S(2)}) collective-permute-start(bf16[1,2048,128]{2,1,0:T(8,128)(2,1)} %get-tuple-element.37), channel_id=1, source_target_pairs={{4,8},{8,4},{5,9},{9,5},{6,10},{10,6},{7,11},{11,7},{20,24},{24,20... | collective-permute-start | bytes 1572872 | tf_op jit(solution)/shard_map/ppermute | solution.py:346
  32.8 6.4 %copy-start = (bf16[1,2048,128]{2,1,0:T(8,128)(2,1)}, bf16[1,2048,128]{2,1,0:T(8,128)(2,1)S(1)}, u32[]{:S(2)}) copy-start(bf16[1,2048,128]{2,1,0:T(8,128)(2,1)S(1)} %collective-permute-done.refs_0_) | copy-start | bytes 1572868
  32.8 6.4 %copy-start.1 = (bf16[1,2048,128]{2,1,0:T(8,128)(2,1)}, bf16[1,2048,128]{2,1,0:T(8,128)(2,1)S(1)}, u32[]{:S(2)}) copy-start(bf16[1,2048,128]{2,1,0:T(8,128)(2,1)S(1)} %collective-permute-done.1.refs_1_) | copy-start | bytes 1572868
  59.0 11.2 %all-to-all-start.1 = ((bf16[32,16,128]{2,1,0:T(8,128)(2,1)}), bf16[32,16,128]{2,1,0:T(8,128)(2,1)S(1)}, u32[]{:S(2)}, u32[]{:S(2)}) async-start(bf16[32,16,128]{2,1,0:T(8,128)(2,1)} %broadcast_in_dim.10), calls=%async_computation.1 | async-start | bytes 262144 | tf_op jit(solution)/shard_map/all_to_all | solution.py:360
where the time goes:
time: 71.5 us; the launch traced here: 71.1 us
  Pallas kernels  24.6 us (34%)
  blocking collectives  19.1 us (27%)
  starting transfers between devices  18.1 us (25%)
  other arithmetic  5.25 us (7%)
  waiting for transfers between devices  1.67 us (2%)
  local copies, waits for them, and re-layouts  1.64 us (2%)
  between operations  0.76 us (1%)
    all_to_all x1, blocking collectives, shards(): swapped = lax.all_to_all(grad, ('dp', 'ctx'), 0, 0, tiled=True)  19.1 us
    pallas_call x1, Pallas kernels, conv(): pl.pallas_call(kernel, grid=(channels // block,), in_specs=[vmem] * (1 +...  11 us
    ppermute x3, starting transfers between devices, shards(): heard.append(lax.ppermute(sent, 'tp', pairs))  7.04 us
    pallas_call x1, Pallas kernels, outer_terms(): pl.pallas_call(kernel, grid=(channels // block,), in_specs=[vmem] * 4, ou...  6.36 us
    pallas_call x1, Pallas kernels, border(): pl.pallas_call(kernel, grid=(channels // block,), in_specs=[halo] * 4 + [...  6.3 us
    select_n x2, other arithmetic, messages(): return (jnp.where(even, u, d), jnp.where(even, d, u))  4.29 us
    ppermute x1, starting transfers between devices, shards(): x2 = lax.ppermute(near_2, 'ctx', near)  4.2 us
    all_to_all x1, starting transfers between devices, shards(): rows = lax.all_to_all(copies, ('dp', 'ctx', 'tp'), 0, 0, tiled=True)  3.19 us
  transfers between devices with their start and end apart: 8, of which 1 were waited for; matrix products, arithmetic and copies ran while one was open for 7% of the time, Pallas kernels for 33%

commit v1 on v0

--- a/solution.py
+++ b/solution.py
@@ -325,6 +325,11 @@
     far = [(i, i + 1) for i in every if i % 2 == 1 and i + 1 < ctx_size]
     far += [(i, i - 1) for i in every if i % 2 == 0 and i > 0]
 
+    up = [i for i in every if i % 2 == 1 and i + 1 < ctx_size]
+    down = [i for i in every if i % 2 == 0 and i > 0]
+    out_hop = [(i, i + 2) for i in up] + [(i, i - 2) for i in down]
+    back_hop = [(i + 2, i + 1) for i in up] + [(i - 2, i - 1) for i in down]
+
     streams = (queries, key_proj, value_proj, grad_output)
     near_1, far_1 = messages(streams, 0, half)
     x1 = lax.ppermute(near_1, "ctx", near)
@@ -342,8 +347,9 @@
 
     *streams_2, _ = lax.optimization_barrier((*streams, near_1))
     near_2, far_2 = messages(streams_2, half, 0)
+    relay = lax.ppermute(far_2, "ctx", out_hop)
     x2 = lax.ppermute(near_2, "ctx", near)
-    d2 = lax.ppermute(far_2, "ctx", far)
+    d2 = lax.ppermute(relay, "ctx", back_hop)
 
     *outs, h, hr, u, d = conv(
         run_ids, heard, owned, queries, key_proj, value_proj, grad_output, members
@@ -352,6 +358,8 @@
     grad = outer_terms(x1, d1, u, d, members, scale)
     outs = border(x1, d1, x2, d2, u, h, hr, queries, key_proj, value_proj, grad_output, outs, members)
 
+    first_heard, *outs = lax.optimization_barrier((heard[0], *outs))
+    heard[0] = first_heard
     slices = dp_size * ctx_size
     each = owned // slices
     swapped = lax.all_to_all(grad, ("dp", "ctx"), 0, 0, tiled=True)

time: 71.5 us -> 68.5 us (0.958)
  blocking collectives: 19.1 us -> 7.43 us
  starting transfers between devices: 18.1 us -> 22.5 us
  waiting for transfers between devices: 1.67 us -> 5.35 us
  Pallas kernels: 24.6 us -> 25.9 us
    all_to_all x1, blocking collectives: 19.1 us -> 7.43 us  [shards(): swapped = lax.all_to_all(grad, ('dp', 'ctx'), 0, 0, tiled=True)]
    ppermute x1 -> x2, starting transfers between devices: 1.46 us -> 4.23 us  [the longest x1 2.95 us: shards(): d2 = lax.ppermute(relay, 'ctx', back_hop)]
    ppermute x3, waiting for transfers between devices: 0.01 us -> 1.99 us  [shards(): heard.append(lax.ppermute(sent, 'tp', pairs))]
    ppermute x1 -> x2, waiting for transfers between devices: 0.01 us -> 1.79 us  [the longest x1 1.79 us: shards(): relay = lax.ppermute(far_2, 'ctx', out_hop)]
    ppermute x1, starting transfers between devices: 1.56 us -> 2.97 us  [shards(): x1 = lax.ppermute(near_1, 'ctx', near)]
    ppermute x3, starting transfers between devices: 7.04 us -> 5.64 us  [shards(): heard.append(lax.ppermute(sent, 'tp', pairs))]
    pallas_call x1, Pallas kernels: 6.36 us -> 7.56 us  [outer_terms(): pl.pallas_call(kernel, grid=(channels // block,), in_specs=[vmem] * 4, ou...]
    convert_element_type x1, other arithmetic: 0.85 us -> 0.01 us  [shards(): sent = jnp.concatenate([filters.astype(NARROW), id_rows], axis=0)]
  transfers between devices with their start and end apart: 8 -> 9, of which waited for: 1 -> 3; matrix products, arithmetic and copies ran while one was open for 7% -> 5% of each run, Pallas kernels for 33% -> 37%
where the time goes in v1:
time: 68.5 us; the launch traced here: 68.1 us
  Pallas kernels  25.9 us (38%)
  starting transfers between devices  22.5 us (33%)
  blocking collectives  7.43 us (11%)
  waiting for transfers between devices  5.35 us (8%)
  other arithmetic  5.23 us (8%)
  local copies, waits for them, and re-layouts  0.94 us (1%)
  between operations  0.78 us (1%)
    pallas_call x1, Pallas kernels, conv(): pl.pallas_call(kernel, grid=(channels // block,), in_specs=[vmem] * (1 +...  11 us
    pallas_call x1, Pallas kernels, outer_terms(): pl.pallas_call(kernel, grid=(channels // block,), in_specs=[vmem] * 4, ou...  7.56 us
    all_to_all x1, blocking collectives, shards(): swapped = lax.all_to_all(grad, ('dp', 'ctx'), 0, 0, tiled=True)  7.43 us
    pallas_call x1, Pallas kernels, border(): pl.pallas_call(kernel, grid=(channels // block,), in_specs=[halo] * 4 + [...  6.39 us
    ppermute x3, starting transfers between devices, shards(): heard.append(lax.ppermute(sent, 'tp', pairs))  5.64 us
    select_n x2, other arithmetic, messages(): return (jnp.where(even, u, d), jnp.where(even, d, u))  5.11 us
    ppermute x1, starting transfers between devices, shards(): x2 = lax.ppermute(near_2, 'ctx', near)  4.23 us
    all_to_all x1, starting transfers between devices, shards(): rows = lax.all_to_all(copies, ('dp', 'ctx', 'tp'), 0, 0, tiled=True)  4.03 us
  transfers between devices with their start and end apart: 9, of which 3 were waited for; matrix products, arithmetic and copies ran while one was open for 5% of the time, Pallas kernels for 37%

profile of v1, /device:TPU:0, one launch (start us, length us, event | category | flops | bytes accessed | tf_op | source)
XLA Modules:
  0.0 68.1 jit_solution(7297182513394749362)
XLA Ops:
  0.6 0.0 copy-start.1
  0.6 0.0 copy-start
  0.7 2.7 %broadcast_select_fusion.2 = (bf16[1,2048,128]{2,1,0:T(8,128)(2,1)}, bf16[1,2048,128]{2,1,0:T(8,128)(2,1)}) fusion(pred[]{:T(512)S(6)} %eq.5, bf16[2,2048,384]{2,1,0:T(8,128)(2,1)} %refs_12_.1, bf16[2,2048,384]{2,1,0:T(8,128)(2,1)} %refs_11_.1, bf16[2,2048,384]{2,1,0:T(8,128)(2,1)} %refs_10_.1, bf16[2,2048,384]{2,1,0:T(8,128)(2,1)} %refs_9_.1), kind=kLoop, calls=%fused_computation.6 | loop fusion | flops 1048576 | bytes 3145729 | tf_op jit(solution)/shard_map/jit(_where)/select_n | solution.py:321
  3.3 3.0 %collective-permute-start = (bf16[1,2048,128]{2,1,0:T(8,128)(2,1)}, bf16[1,2048,128]{2,1,0:T(8,128)(2,1)}, u32[]{:S(2)}, u32[]{:S(2)}) collective-permute-start(bf16[1,2048,128]{2,1,0:T(8,128)(2,1)} %get-tuple-element.50), channel_id=1, source_target_pairs={{0,4},{4,0},{8,12},{12,8},{1,5},{5,1},{9,13},{13,9},{2,6},{6,2},{1... | collective-permute-start | bytes 1572872 | tf_op jit(solution)/shard_map/ppermute | solution.py:335
  6.3 1.4 %collective-permute-start.1 = (bf16[1,2048,128]{2,1,0:T(8,128)(2,1)}, bf16[1,2048,128]{2,1,0:T(8,128)(2,1)}, u32[]{:S(2)}, u32[]{:S(2)}) collective-permute-start(bf16[1,2048,128]{2,1,0:T(8,128)(2,1)} %get-tuple-element.49), channel_id=1, source_target_pairs={{4,8},{8,4},{5,9},{9,5},{6,10},{10,6},{7,11},{11,7},{20,24},{24,20... | collective-permute-start | bytes 1572872 | tf_op jit(solution)/shard_map/ppermute | solution.py:336
  7.7 2.5 %broadcast_select_fusion = (bf16[1,2048,128]{2,1,0:T(8,128)(2,1)S(1)}, bf16[1,2048,128]{2,1,0:T(8,128)(2,1)}) fusion(pred[]{:T(512)S(6)} %eq.5, bf16[2,2048,384]{2,1,0:T(8,128)(2,1)} %refs_12_.1, bf16[2,2048,384]{2,1,0:T(8,128)(2,1)} %refs_11_.1, bf16[2,2048,384]{2,1,0:T(8,128)(2,1)} %refs_10_.1, bf16[2,2048,384]{2,1,0:T(8,128)(2,1)} %refs_9_.1), kind=kLoop, calls=%fused_computation.4 | loop fusion | flops 1048576 | bytes 3145729 | tf_op jit(solution)/shard_map/jit(_where)/select_n | solution.py:321
  10.2 1.3 %collective-permute-start.3 = (bf16[1,2048,128]{2,1,0:T(8,128)(2,1)S(1)}, bf16[1,2048,128]{2,1,0:T(8,128)(2,1)}, u32[]{:S(2)}, u32[]{:S(2)}) collective-permute-start(bf16[1,2048,128]{2,1,0:T(8,128)(2,1)S(1)} %get-tuple-element.47), channel_id=1, source_target_pairs={{4,12},{8,0},{5,13},{9,1},{6,14},{10,2},{7,15},{11,3},{20,28},{24,... | collective-permute-start | bytes 1572872 | tf_op jit(solution)/shard_map/ppermute | solution.py:350
  11.5 0.0 copy-done.1
  11.5 0.1 reshape.163
  11.6 0.1 slice_reduce_fusion
  11.7 0.0 copy-done
  11.7 0.1 pad.3.clone
  11.8 0.1 maximum_maximum_fusion.refs_1_.refs_0_
  11.9 1.6 %collective-permute-start.5 = (bf16[144,128]{1,0:T(8,128)(2,1)S(1)}, bf16[144,128]{1,0:T(8,128)(2,1)S(1)}, u32[]{:S(2)}, u32[]{:S(2)}) collective-permute-start(bf16[144,128]{1,0:T(8,128)(2,1)S(1)} %maximum_maximum_fusion.refs_1_.refs_0_), channel_id=1, source_target_pairs={{0,1},{1,2},{2,3},{3,0},{4,5},{5,6},{6,7},{7,4},{8,9},{9,10},{10,1... | collective-permute-start | bytes 110600 | tf_op jit(solution)/shard_map/ppermute | solution.py:346
  13.5 2.6 %collective-permute-start.6 = (bf16[144,128]{1,0:T(8,128)(2,1)S(1)}, bf16[144,128]{1,0:T(8,128)(2,1)S(1)}, u32[]{:S(2)}, u32[]{:S(2)}) collective-permute-start(bf16[144,128]{1,0:T(8,128)(2,1)S(1)} %maximum_maximum_fusion.refs_1_.refs_0_), channel_id=1, source_target_pairs={{0,2},{1,3},{2,0},{3,1},{4,6},{5,7},{6,4},{7,5},{8,10},{9,11},{10,... | collective-permute-start | bytes 110600 | tf_op jit(solution)/shard_map/ppermute | solution.py:346
  16.1 2.0 %collective-permute-done.5.refs_2_.refs_1_ = bf16[144,128]{1,0:T(8,128)(2,1)S(1)} collective-permute-done((bf16[144,128]{1,0:T(8,128)(2,1)S(1)}, bf16[144,128]{1,0:T(8,128)(2,1)S(1)}, u32[]{:S(2)}, u32[]{:S(2)}) %collective-permute-start.5) | collective-permute-done | bytes 36896 | tf_op jit(solution)/shard_map/ppermute | solution.py:346
  18.1 1.4 %collective-permute-start.7 = (bf16[144,128]{1,0:T(8,128)(2,1)S(1)}, bf16[144,128]{1,0:T(8,128)(2,1)S(1)}, u32[]{:S(2)}, u32[]{:S(2)}) collective-permute-start(bf16[144,128]{1,0:T(8,128)(2,1)S(1)} %maximum_maximum_fusion.refs_1_.refs_0_), channel_id=1, source_target_pairs={{0,3},{1,0},{2,1},{3,2},{4,7},{5,4},{6,5},{7,6},{8,11},{9,8},{10,9... | collective-permute-start | bytes 110600 | tf_op jit(solution)/shard_map/ppermute | solution.py:346
  19.5 0.0 collective-permute-done.6.refs_3_.refs_2_
  19.5 4.2 %collective-permute-start.2 = (bf16[1,2048,128]{2,1,0:T(8,128)(2,1)}, bf16[1,2048,128]{2,1,0:T(8,128)(2,1)}, u32[]{:S(2)}, u32[]{:S(2)}) collective-permute-start(bf16[1,2048,128]{2,1,0:T(8,128)(2,1)} %get-tuple-element.48), channel_id=1, source_target_pairs={{0,4},{4,0},{8,12},{12,8},{1,5},{5,1},{9,13},{13,9},{2,6},{6,2},{1... | collective-permute-start | bytes 1572872 | tf_op jit(solution)/shard_map/ppermute | solution.py:351
  23.8 1.8 %collective-permute-done.3 = bf16[1,2048,128]{2,1,0:T(8,128)(2,1)} collective-permute-done((bf16[1,2048,128]{2,1,0:T(8,128)(2,1)S(1)}, bf16[1,2048,128]{2,1,0:T(8,128)(2,1)}, u32[]{:S(2)}, u32[]{:S(2)}) %collective-permute-start.3) | collective-permute-done | bytes 524320 | tf_op jit(solution)/shard_map/ppermute | solution.py:350
  25.5 3.0 %collective-permute-start.4 = (bf16[1,2048,128]{2,1,0:T(8,128)(2,1)}, bf16[1,2048,128]{2,1,0:T(8,128)(2,1)}, u32[]{:S(2)}, u32[]{:S(2)}) collective-permute-start(bf16[1,2048,128]{2,1,0:T(8,128)(2,1)} %collective-permute-done.3), channel_id=1, source_target_pairs={{12,8},{0,4},{13,9},{1,5},{14,10},{2,6},{15,11},{3,7},{28,24},{16,... | collective-permute-start | bytes 1572872 | tf_op jit(solution)/shard_map/ppermute | solution.py:352
  28.5 0.0 collective-permute-done.7.refs_4_.refs_3_
  28.5 11.0 %conv.1 = (bf16[2,2048,384]{2,1,0:T(8,128)(2,1)}, bf16[2,2048,384]{2,1,0:T(8,128)(2,1)}, bf16[2,2048,384]{2,1,0:T(8,128)(2,1)}, bf16[2,2048,384]{2,1,0:T(8,128)(...) custom-call(s32[1,128]{1,0:T(1,128)S(1)} %bitcast.11, ...), custom_call_target="tpu_custom_call" | custom-call | flops 1610612736 | bytes 25165824 | tf_op jit(solution)/shard_map/conv/pallas_call | solution.py:129
  39.5 0.0 collective-permute-done.refs_0_
  39.5 0.0 collective-permute-done.1.refs_1_
  39.5 7.6 %outer.1 = f32[128,128]{1,0:T(8,128)S(1)} custom-call(bf16[1,2048,128]{2,1,0:T(8,128)(2,1)} %collective-permute-done.refs_0_, bf16[1,2048,128]{2,1,0:T(8,128)(2,1)} %collective-permute-done.1.refs_1_, bf16[2,2048,384]{2,1,0:T(8,128)(2,1)S(1)} %get-tuple-element.30.refs_4_.refs_2_, bf16[2,2048,384]{2,1,0:T(8,128)(2,1)S(1)} %get-tuple-element.46.refs_3_), custom_call_target="tpu_custom_call" | custom-call | flops 1610612736 | bytes 12582912 | tf_op jit(solution)/shard_map/outer/pallas_call | solution.py:201
  47.0 7.4 %all_to_all.14 = f32[8,16,128]{2,1,0:T(8,128)S(1)} all-to-all(f32[8,16,128]{2,1,0:T(8,128)S(1)} %bitcast.10), channel_id=1, replica_groups=mesh['dp'=2,'ctx'=4,'tp'=4] {'dp','ctx'}, dimensions={0} | all-to-all | bytes 131072 | tf_op jit(solution)/shard_map/all_to_all | solution.py:365
  54.5 0.7 broadcast_in_dim.10
  55.2 4.0 %all-to-all-start.1 = ((bf16[32,16,128]{2,1,0:T(8,128)(2,1)}), bf16[32,16,128]{2,1,0:T(8,128)(2,1)S(1)}, u32[]{:S(2)}, u32[]{:S(2)}) async-start(bf16[32,16,128]{2,1,0:T(8,128)(2,1)} %broadcast_in_dim.10), calls=%async_computation.1 | async-start | bytes 262144 | tf_op jit(solution)/shard_map/all_to_all | solution.py:368
  59.2 0.0 collective-permute-done.2.refs_2_
  59.2 0.0 collective-permute-done.4.refs_3_
  59.2 6.4 %border.1 = (bf16[2,2048,384]{2,1,0:T(8,128)(2,1)}, bf16[2,2048,384]{2,1,0:T(8,128)(2,1)}, bf16[2,2048,384]{2,1,0:T(8,128)(2,1)}, bf16[2,2048,384]{2,1,0:T(8,128)(2,1)}) custom-call(bf16[1,2048,128]{2,1,0:T(8,128)(2,1)} %collective-permute-done.refs_0_, ...), custom_call_target="tpu_custom_call", output_to_operand_aliasing={{0}: (13, {}), {1}: (14, {}), {2}: (15, {}), {3}: (16, {})} | custom-call | flops 1073741824 | bytes 16777216 | tf_op jit(solution)/shard_map/border/pallas_call | solution.py:267
  65.6 1.6 %all-to-all-done.1 = bf16[32,16,128]{2,1,0:T(8,128)(2,1)S(1)} async-done(((bf16[32,16,128]{2,1,0:T(8,128)(2,1)}), bf16[32,16,128]{2,1,0:T(8,128)(2,1)S(1)}, u32[]{:S(2)}, u32[]{:S(2)}) %all-to-all-start.1) | async-done | bytes 131104 | tf_op jit(solution)/shard_map/all_to_all | solution.py:368
  67.2 0.9 %place.1 = f32[128,128]{1,0:T(8,128)} custom-call(bf16[144,128]{1,0:T(8,128)(2,1)S(1)} %maximum_maximum_fusion.refs_1_.refs_0_, bf16[144,128]{1,0:T(8,128)(2,1)S(1)} %collective-permute-done.5.refs_2_.refs_1_, bf16[144,128]{1,0:T(8,128)(2,1)S(1)} %collective-permute-done.6.refs_3_.refs_2_, bf16[144,128]{1,0:T(8,128)(2,1)S(1)} %collective-permute-done.7.refs_4_.refs_3_, ...), custom_call_target="tpu_custom_call" | custom-call | tf_op jit(solution)/shard_map/place/pallas_call | solution.py:374
  (4 shorter events, 0.0 us)
Async XLA Ops:
  0.6 10.8 %copy-start.1 = (s32[2048]{0:T(1024)S(1)}, s32[2048]{0:T(1024)}, u32[]{:S(2)}) copy-start(s32[2048]{0:T(1024)} %param.11) | copy-start | bytes 24580
  0.6 11.0 %copy-start = (f32[128,128]{1,0:T(8,128)S(1)}, f32[128,128]{1,0:T(8,128)}, u32[]{:S(2)}) copy-start(f32[128,128]{1,0:T(8,128)} %param.10) | copy-start | bytes 196612
  3.3 36.1 %collective-permute-start = (bf16[1,2048,128]{2,1,0:T(8,128)(2,1)}, bf16[1,2048,128]{2,1,0:T(8,128)(2,1)}, u32[]{:S(2)}, u32[]{:S(2)}) collective-permute-start(bf16[1,2048,128]{2,1,0:T(8,128)(2,1)} %get-tuple-element.50), channel_id=1, source_target_pairs={{0,4},{4,0},{8,12},{12,8},{1,5},{5,1},{9,13},{13,9},{2,6},{6,2},{1... | collective-permute-start | bytes 1572872 | tf_op jit(solution)/shard_map/ppermute | solution.py:335
  6.3 33.2 %collective-permute-start.1 = (bf16[1,2048,128]{2,1,0:T(8,128)(2,1)}, bf16[1,2048,128]{2,1,0:T(8,128)(2,1)}, u32[]{:S(2)}, u32[]{:S(2)}) collective-permute-start(bf16[1,2048,128]{2,1,0:T(8,128)(2,1)} %get-tuple-element.49), channel_id=1, source_target_pairs={{4,8},{8,4},{5,9},{9,5},{6,10},{10,6},{7,11},{11,7},{20,24},{24,20... | collective-permute-start | bytes 1572872 | tf_op jit(solution)/shard_map/ppermute | solution.py:336
  10.2 15.4 %collective-permute-start.3 = (bf16[1,2048,128]{2,1,0:T(8,128)(2,1)S(1)}, bf16[1,2048,128]{2,1,0:T(8,128)(2,1)}, u32[]{:S(2)}, u32[]{:S(2)}) collective-permute-start(bf16[1,2048,128]{2,1,0:T(8,128)(2,1)S(1)} %get-tuple-element.47), channel_id=1, source_target_pairs={{4,12},{8,0},{5,13},{9,1},{6,14},{10,2},{7,15},{11,3},{20,28},{24,... | collective-permute-start | bytes 1572872 | tf_op jit(solution)/shard_map/ppermute | solution.py:350
  11.9 6.2 %collective-permute-start.5 = (bf16[144,128]{1,0:T(8,128)(2,1)S(1)}, bf16[144,128]{1,0:T(8,128)(2,1)S(1)}, u32[]{:S(2)}, u32[]{:S(2)}) collective-permute-start(bf16[144,128]{1,0:T(8,128)(2,1)S(1)} %maximum_maximum_fusion.refs_1_.refs_0_), channel_id=1, source_target_pairs={{0,1},{1,2},{2,3},{3,0},{4,5},{5,6},{6,7},{7,4},{8,9},{9,10},{10,1... | collective-permute-start | bytes 110600 | tf_op jit(solution)/shard_map/ppermute | solution.py:346
  13.5 6.0 %collective-permute-start.6 = (bf16[144,128]{1,0:T(8,128)(2,1)S(1)}, bf16[144,128]{1,0:T(8,128)(2,1)S(1)}, u32[]{:S(2)}, u32[]{:S(2)}) collective-permute-start(bf16[144,128]{1,0:T(8,128)(2,1)S(1)} %maximum_maximum_fusion.refs_1_.refs_0_), channel_id=1, source_target_pairs={{0,2},{1,3},{2,0},{3,1},{4,6},{5,7},{6,4},{7,5},{8,10},{9,11},{10,... | collective-permute-start | bytes 110600 | tf_op jit(solution)/shard_map/ppermute | solution.py:346
  18.1 10.4 %collective-permute-start.7 = (bf16[144,128]{1,0:T(8,128)(2,1)S(1)}, bf16[144,128]{1,0:T(8,128)(2,1)S(1)}, u32[]{:S(2)}, u32[]{:S(2)}) collective-permute-start(bf16[144,128]{1,0:T(8,128)(2,1)S(1)} %maximum_maximum_fusion.refs_1_.refs_0_), channel_id=1, source_target_pairs={{0,3},{1,0},{2,1},{3,2},{4,7},{5,4},{6,5},{7,6},{8,11},{9,8},{10,9... | collective-permute-start | bytes 110600 | tf_op jit(solution)/shard_map/ppermute | solution.py:346
  19.5 39.7 %collective-permute-start.2 = (bf16[1,2048,128]{2,1,0:T(8,128)(2,1)}, bf16[1,2048,128]{2,1,0:T(8,128)(2,1)}, u32[]{:S(2)}, u32[]{:S(2)}) collective-permute-start(bf16[1,2048,128]{2,1,0:T(8,128)(2,1)} %get-tuple-element.48), channel_id=1, source_target_pairs={{0,4},{4,0},{8,12},{12,8},{1,5},{5,1},{9,13},{13,9},{2,6},{6,2},{1... | collective-permute-start | bytes 1572872 | tf_op jit(solution)/shard_map/ppermute | solution.py:351
  25.5 33.7 %collective-permute-start.4 = (bf16[1,2048,128]{2,1,0:T(8,128)(2,1)}, bf16[1,2048,128]{2,1,0:T(8,128)(2,1)}, u32[]{:S(2)}, u32[]{:S(2)}) collective-permute-start(bf16[1,2048,128]{2,1,0:T(8,128)(2,1)} %collective-permute-done.3), channel_id=1, source_target_pairs={{12,8},{0,4},{13,9},{1,5},{14,10},{2,6},{15,11},{3,7},{28,24},{16,... | collective-permute-start | bytes 1572872 | tf_op jit(solution)/shard_map/ppermute | solution.py:352
  55.2 12.0 %all-to-all-start.1 = ((bf16[32,16,128]{2,1,0:T(8,128)(2,1)}), bf16[32,16,128]{2,1,0:T(8,128)(2,1)S(1)}, u32[]{:S(2)}, u32[]{:S(2)}) async-start(bf16[32,16,128]{2,1,0:T(8,128)(2,1)} %broadcast_in_dim.10), calls=%async_computation.1 | async-start | bytes 262144 | tf_op jit(solution)/shard_map/all_to_all | solution.py:368
